TPU v7x, 32 devices: a whole 2x2x4 slice. The times are simulated.
32 devices in a mesh: parts: 2 (over x), chol: 16 (over z, y, core).
Axes of the slice: x: 2, y: 2, z: 4, core: 2. Of those that a mesh axis runs over, the one named last changes fastest.
Arguments:
- orbitals: float32 [32, 100, 1024], P(('parts', 'chol')), parts along dimension 0, may hold values from -6 to 6
- intersection_inv: float32 [32, 100, 100], P(('parts', 'chol')), parts along dimension 0, may hold values from -0.625 to 0.625
- factor_rows: bfloat16 [4096, 1024], P('chol'), may hold values from -0.1875 to 0.1875
- factor_rotated: bfloat16 [100, 4096], replicated, may hold values from -0.625 to 0.625
- factor_core: bfloat16 [1024, 4096], P('chol'), may hold values from -0.125 to 0.125
- fields: float32 [32, 1024], P('parts', 'chol'), parts along dimension 0, may hold values from -6 to 6
Outputs:
- propagated: float32 [32, 100, 1024], P(('parts', 'chol')), parts along dimension 0
- force_bias: float32 [32, 1024], P('parts', 'chol'), parts along dimension 0
There are 2 independent parts, one for each index of `parts`. A program takes and returns all parts, laid end to end along the dimension named above; an argument that names none is the same for every part. Nothing has to cross between parts.
All inputs are finite; a program needn't handle non-finite values.
Results may differ from a plain program's by a relative error of at most 0.0091.
Values may be sent and summed in bfloat16 or wider, within the bound.
A program may use at most 64 MiB of HBM per device.

v0:
```python
import jax
import jax.numpy as jnp
from jax import lax
from jax.sharding import PartitionSpec as P

TAYLOR = 4


def density_one(half_green, all_rows, factor_rotated):
    projected = lax.dot_general(
        half_green, all_rows, (((1,), (1,)), ((), ())), preferred_element_type=jnp.float32
    )
    return jnp.sum(factor_rotated.astype(jnp.float32) * projected, axis=0).astype(jnp.bfloat16)


def propagate_one(orbital, potential, all_rows):
    total = orbital
    term = orbital
    for order in range(1, TAYLOR + 1):
        summed = lax.dot_general(
            term.astype(jnp.bfloat16),
            all_rows,
            (((1,), (1,)), ((), ())),
            preferred_element_type=jnp.float32,
        )
        scaled = (summed * potential[None, :] / order).astype(jnp.bfloat16)
        term = jnp.dot(scaled, all_rows, preferred_element_type=jnp.float32)
        total = total + term
    return total


def on_device(orbitals, intersection_inv, factor_rows, factor_rotated, factor_core, fields):
    walker_count = orbitals.shape[0]
    half_green = jnp.einsum(
        "wij,wjm->wim", intersection_inv, orbitals, precision=lax.Precision.HIGHEST
    ).astype(jnp.bfloat16)
    all_rows = lax.all_gather(factor_rows, "chol", axis=0, tiled=True)
    own_density = lax.map(lambda item: density_one(item, all_rows, factor_rotated), half_green)
    density = lax.all_gather(own_density, "chol", axis=0, tiled=True)
    force_bias = lax.dot_general(
        density, factor_core, (((1,), (1,)), ((), ())), preferred_element_type=jnp.float32
    )
    shifted = (fields - force_bias).astype(jnp.bfloat16)
    partial_sum = jnp.dot(shifted, factor_core, preferred_element_type=jnp.float32)
    summed_all = lax.psum(partial_sum, "chol")
    potential = lax.dynamic_slice_in_dim(
        summed_all, lax.axis_index("chol") * walker_count, walker_count, 0
    )
    propagated = lax.map(
        lambda pair: propagate_one(pair[0], pair[1], all_rows), (orbitals, potential)
    )
    return (propagated, force_bias)


def solution(mesh):
    in_specs = (
        P(("parts", "chol"), None, None),
        P(("parts", "chol"), None, None),
        P("chol", None),
        P(),
        P("chol", None),
        P("parts", "chol"),
    )
    out_specs = (P(("parts", "chol"), None, None), P("parts", "chol"))
    return jax.shard_map(
        on_device, mesh=mesh, in_specs=in_specs, out_specs=out_specs, check_vma=False
    )
```

profile of v0, /device:TPU:0, one launch (start us, length us, event | category | flops | bytes accessed | tf_op | source)
XLA Modules:
  0.0 249.2 jit_solution(8666170632495442712)
XLA Ops:
  7.2 0.0 copy-start
  7.2 0.0 copy-start.1
  7.2 0.0 copy-start.3
  7.2 0.0 all-gather.3.cloned.1.call-start
  7.2 0.7 all-gather.3.cloned.1.call-update
  7.9 0.0 all-reduce.2.cloned.1.call-start
  8.0 1.6 convolution_convert_fusion
  9.6 77.7 %all-gather.3.cloned.1.call-done = bf16[4096,1024]{1,0:T(8,128)(2,1)} async-done(((bf16[256,1024]{1,0:T(8,128)(2,1)}), bf16[4096,1024]{1,0:T(8,128)(2,1)}) %all-gather.3.cloned.1.call-update) | async-done | bytes 8388624 | tf_op jit(solution)/shard_map/all_gather | solution.py:37
  87.2 6.3 %fusion.7 = bf16[4096]{0:T(1024)(128)(2,1)S(1)} fusion(bf16[100,1024]{1,0:T(8,128)(2,1)S(1)} %convolution_convert_fusion, bf16[4096,1024]{1,0:T(8,128)(2,1)} %all-gather.3.cloned.1.call-done, bf16[100,4096]{1,0:T(8,128)(2,1)} %param.9), kind=kOutput, calls=%fused_computation.12 | convolution fusion | flops 840085504 | bytes 9420800 | tf_op jit(solution)/shard_map/while/body/eval_jaxpr/dot_general | solution.py:10
  93.5 19.5 %all-gather = bf16[65536]{0:T(1024)(128)(2,1)S(1)} all-gather(bf16[4096]{0:T(1024)(128)(2,1)S(1)} %fusion.7), channel_id=2, replica_groups=mesh['parts'=2,'chol'=16] {'chol'}, dimensions={0}, use_global_device_ids=true | all-gather | bytes 139264 | tf_op jit(solution)/shard_map/all_gather | solution.py:39
  113.0 0.1 reshape.20
  113.1 0.0 copy-done
  113.1 0.2 fusion.28
  113.3 0.9 fusion.24
  114.2 0.0 all-reduce.2.cloned.1.call-update
  114.3 87.1 %all-reduce.2.cloned.1.call-done = f32[16,4096]{1,0:T(8,128)} async-done(((f32[16,4096]{1,0:T(8,128)}), f32[16,4096]{1,0:T(8,128)}) %all-reduce.2.cloned.1.call-update) | async-done | bytes 262160 | tf_op jit(solution)/shard_map/psum | solution.py:45
  201.4 0.9 constant_dynamic-slice_fusion
  202.3 0.0 copy-done.1
  202.3 9.7 %fusion.11 = f32[100,1024]{1,0:T(8,128)S(1)} fusion(bf16[4096,1024]{1,0:T(8,128)(2,1)} %all-gather.3.cloned.1.call-done, f32[4096]{0:T(1024)S(1)} %bitcast.32, f32[1,100,1024]{2,0,1:T(1,128)S(1)} %copy-done.1), kind=kOutput, calls=%fused_computation.18 | convolution fusion | flops 1678540800 | bytes 9224192 | tf_op jit(solution)/shard_map/while/body/eval_jaxpr/dot_general | solution.py:27
  212.0 0.0 copy-done.2
  212.0 9.7 %fusion.10 = f32[100,1024]{1,0:T(8,128)S(1)} fusion(bf16[4096,1024]{1,0:T(8,128)(2,1)} %all-gather.3.cloned.1.call-done, f32[4096]{0:T(1024)S(1)} %bitcast.33, f32[100,1024]{1,0:T(8,128)S(1)} %fusion.11), kind=kOutput, calls=%fused_computation.17 | convolution fusion | flops 1679052800 | bytes 9224192 | tf_op jit(solution)/shard_map/while/body/eval_jaxpr/dot_general | solution.py:27
  221.7 9.7 %fusion.9 = f32[100,1024]{1,0:T(8,128)S(1)} fusion(bf16[4096,1024]{1,0:T(8,128)(2,1)} %all-gather.3.cloned.1.call-done, f32[4096]{0:T(1024)S(1)} %bitcast.34, f32[100,1024]{1,0:T(8,128)S(1)} %fusion.10), kind=kOutput, calls=%fused_computation.16 | convolution fusion | flops 1679052800 | bytes 9224192 | tf_op jit(solution)/shard_map/while/body/eval_jaxpr/dot_general | solution.py:27
  231.5 9.7 %fusion.8 = f32[1,100,1024]{2,1,0:T(8,128)S(1)} fusion(bf16[4096,1024]{1,0:T(8,128)(2,1)} %all-gather.3.cloned.1.call-done, f32[4096]{0:T(1024)S(1)} %bitcast.35, f32[100,1024]{1,0:T(8,128)S(1)} %fusion.9, f32[100,1024]{1,0:T(8,128)S(1)} %fusion.10, f32[100,1024]{1,0:T(8,128)S(1)} %fusion.11, f32[1,100,1024]{2,0,1:T(1,128)S(1)} %copy-done.1), kind=kOutput, calls=%fused_computation.14 | convolution fusion | flops 1679462400 | bytes 10452992 | tf_op jit(solution)/shard_map/while/body/eval_jaxpr/dot_general | solution.py:27
  241.2 1.2 copy.9
  (2 shorter events, 0.0 us)
Async XLA Ops:
  7.2 105.9 %copy-start = (bf16[64,4096]{1,0:T(8,128)(2,1)S(1)}, bf16[64,4096]{1,0:T(8,128)(2,1)}, u32[]{:S(2)}) copy-start(bf16[64,4096]{1,0:T(8,128)(2,1)} %param.10) | copy-start | bytes 1572868
  7.2 195.2 %copy-start.1 = (f32[1,100,1024]{2,0,1:T(1,128)S(1)}, f32[1,100,1024]{2,0,1:T(1,128)}, u32[]{:S(2)}) copy-start(f32[1,100,1024]{2,0,1:T(1,128)} %param.6) | copy-start | bytes 1228804
  7.2 106.1 %copy-start.3 = (f32[16,64]{1,0:T(8,128)S(1)}, f32[16,64]{1,0:T(8,128)}, u32[]{:S(2)}) copy-start(f32[16,64]{1,0:T(8,128)} %param.11) | copy-start | bytes 12292
  7.2 80.0 %all-gather.3.cloned.1.call-start = ((), (), s32[]{:S(2)}) async-start(), calls=%async_computation | async-start | bytes 8912896 | tf_op jit(solution)/shard_map/all_gather | solution.py:37
  7.9 193.5 %all-reduce.2.cloned.1.call-start = ((), (), s32[]{:S(2)}) async-start(), calls=%async_computation.1 | async-start | bytes 524288 | tf_op jit(solution)/shard_map/psum | solution.py:45
  113.3 98.7 %copy-start.2 = (f32[16,64]{1,0:T(8,128)}, f32[16,64]{1,0:T(8,128)S(1)}, u32[]{:S(2)}) copy-start(f32[16,64]{1,0:T(8,128)S(1)} %fusion.28) | copy-start | bytes 12292
Sparse Core Ops, SparseCore 0:
  10.2 77.0 all-gather.2
  114.4 86.9 all-reduce.1
where the time goes:
time: 249 us
  waiting for transfers between devices  166 us (67%)
  matrix products  47.9 us (19%)
  blocking collectives  19.5 us (8%)
  between operations  14.1 us (6%)
    psum x1, waiting for transfers between devices, on_device(): summed_all = lax.psum(partial_sum, 'chol')  87.1 us
    all_gather x1, waiting for transfers between devices, on_device(): all_rows = lax.all_gather(factor_rows, 'chol', axis=0, tiled=True)  77.7 us
    dot_general x4, matrix products, propagate_one(): term = jnp.dot(scaled, all_rows, preferred_element_type=jnp.float32)  38.9 us
    all_gather x1, blocking collectives, on_device(): density = lax.all_gather(own_density, 'chol', axis=0, tiled=True)  19.5 us
    dot_general x1, matrix products, density_one(): lax.dot_general(half_green, all_rows, (((1,), (1,)), ((), ())), preferred...  6.26 us
  transfers between devices with their start and end apart: 2, of which 2 were waited for; matrix products, arithmetic and copies ran while one was open for 1% of the time, Pallas kernels for 0%

commit v1 on v0

--- a/solution.py
+++ b/solution.py
@@ -42,7 +42,7 @@
     )
     shifted = (fields - force_bias).astype(jnp.bfloat16)
     partial_sum = jnp.dot(shifted, factor_core, preferred_element_type=jnp.float32)
-    summed_all = lax.psum(partial_sum, "chol")
+    summed_all = jnp.sum(lax.all_gather(partial_sum, "chol"), axis=0)
     potential = lax.dynamic_slice_in_dim(
         summed_all, lax.axis_index("chol") * walker_count, walker_count, 0
     )

time: 249 us -> 212 us (0.85)
  waiting for transfers between devices: 166 us -> 126 us
    psum x1 -> x0, waiting for transfers between devices: 87.1 us -> none  [on_device(): summed_all = lax.psum(partial_sum, 'chol')]
    all_gather x0 -> x1, waiting for transfers between devices: none -> 47.8 us  [on_device(): summed_all = jnp.sum(lax.all_gather(partial_sum, 'chol'), axis=0)]
where the time goes in v1:
time: 212 us; the launch traced here: 211 us
  waiting for transfers between devices  126 us (59%)
  matrix products  47.9 us (23%)
  blocking collectives  19.5 us (9%)
  between operations  14.1 us (7%)
  other arithmetic  2.4 us (1%)
    all_gather x1, waiting for transfers between devices, on_device(): all_rows = lax.all_gather(factor_rows, 'chol', axis=0, tiled=True)  77.6 us
    all_gather x1, waiting for transfers between devices, on_device(): summed_all = jnp.sum(lax.all_gather(partial_sum, 'chol'), axis=0)  47.8 us
    dot_general x4, matrix products, propagate_one(): term = jnp.dot(scaled, all_rows, preferred_element_type=jnp.float32)  38.8 us
    all_gather x1, blocking collectives, on_device(): density = lax.all_gather(own_density, 'chol', axis=0, tiled=True)  19.5 us
    dot_general x1, matrix products, density_one(): lax.dot_general(half_green, all_rows, (((1,), (1,)), ((), ())), preferred...  6.26 us
  transfers between devices with their start and end apart: 2, of which 2 were waited for; matrix products, arithmetic and copies ran while one was open for 1% of the time, Pallas kernels for 0%

profile of v1, /device:TPU:0, one launch (start us, length us, event | category | flops | bytes accessed | tf_op | source)
XLA Modules:
  0.0 211.3 jit_solution(13803351827885669895)
XLA Ops:
  7.2 0.0 copy-start
  7.2 0.0 copy-start.3
  7.2 0.0 all-gather.5.cloned.1.call-start
  7.2 0.7 all-gather.5.cloned.1.call-update
  7.9 0.0 copy-start.1
  7.9 0.0 all-gather.7.cloned.1.call-start
  8.0 1.6 convolution_convert_fusion
  9.6 77.6 %all-gather.5.cloned.1.call-done = bf16[4096,1024]{1,0:T(8,128)(2,1)} async-done(((bf16[256,1024]{1,0:T(8,128)(2,1)}), bf16[4096,1024]{1,0:T(8,128)(2,1)}) %all-gather.5.cloned.1.call-update) | async-done | bytes 8388624 | tf_op jit(solution)/shard_map/all_gather | solution.py:37
  87.2 6.3 %fusion.7 = bf16[4096]{0:T(1024)(128)(2,1)S(1)} fusion(bf16[100,1024]{1,0:T(8,128)(2,1)S(1)} %convolution_convert_fusion, bf16[4096,1024]{1,0:T(8,128)(2,1)} %all-gather.5.cloned.1.call-done, bf16[100,4096]{1,0:T(8,128)(2,1)} %param.9), kind=kOutput, calls=%fused_computation.12 | convolution fusion | flops 840085504 | bytes 9420800 | tf_op jit(solution)/shard_map/while/body/eval_jaxpr/dot_general | solution.py:10
  93.5 19.5 %all-gather = bf16[65536]{0:T(1024)(128)(2,1)S(1)} all-gather(bf16[4096]{0:T(1024)(128)(2,1)S(1)} %fusion.7), channel_id=2, replica_groups=mesh['parts'=2,'chol'=16] {'chol'}, dimensions={0}, use_global_device_ids=true | all-gather | bytes 139264 | tf_op jit(solution)/shard_map/all_gather | solution.py:39
  113.0 0.1 reshape.20
  113.1 0.0 copy-done
  113.1 0.2 fusion.28
  113.3 0.0 copy-done.3
  113.3 0.9 fusion.24
  114.2 0.0 all-gather.7.cloned.1.call-update
  114.3 47.8 %all-gather.7.cloned.1.call-done = f32[256,4096]{1,0:T(8,128)} async-done(((f32[16,4096]{1,0:T(8,128)}), f32[256,4096]{1,0:T(8,128)}) %all-gather.7.cloned.1.call-update) | async-done | bytes 4194320 | tf_op jit(solution)/shard_map/all_gather | solution.py:45
  162.0 2.4 %reduce_sum.20 = f32[16,4096]{1,0:T(8,128)S(1)} reduce(f32[16,16,4096]{2,1,0:T(8,128)} %bitcast.33, f32[]{:T(128)} %constant.24.clone.1), dimensions={0}, to_apply=%region_1.0 | reduce | flops 983040 | bytes 4456452 | tf_op jit(solution)/shard_map/reduce_sum | solution.py:45
  164.5 0.0 copy-done.1
  164.5 9.7 %fusion.11 = f32[100,1024]{1,0:T(8,128)S(1)} fusion(bf16[4096,1024]{1,0:T(8,128)(2,1)} %all-gather.5.cloned.1.call-done, f32[4096]{0:T(1024)S(1)} %bitcast.34, f32[1,100,1024]{2,0,1:T(1,128)S(1)} %copy-done.1), kind=kOutput, calls=%fused_computation.18 | convolution fusion | flops 1678540800 | bytes 9224192 | tf_op jit(solution)/shard_map/while/body/eval_jaxpr/dot_general | solution.py:27
  174.2 9.7 %fusion.10 = f32[100,1024]{1,0:T(8,128)S(1)} fusion(bf16[4096,1024]{1,0:T(8,128)(2,1)} %all-gather.5.cloned.1.call-done, f32[4096]{0:T(1024)S(1)} %bitcast.35, f32[100,1024]{1,0:T(8,128)S(1)} %fusion.11), kind=kOutput, calls=%fused_computation.17 | convolution fusion | flops 1679052800 | bytes 9224192 | tf_op jit(solution)/shard_map/while/body/eval_jaxpr/dot_general | solution.py:27
  183.8 9.7 %fusion.9 = f32[100,1024]{1,0:T(8,128)S(1)} fusion(bf16[4096,1024]{1,0:T(8,128)(2,1)} %all-gather.5.cloned.1.call-done, f32[4096]{0:T(1024)S(1)} %bitcast.36, f32[100,1024]{1,0:T(8,128)S(1)} %fusion.10), kind=kOutput, calls=%fused_computation.16 | convolution fusion | flops 1679052800 | bytes 9224192 | tf_op jit(solution)/shard_map/while/body/eval_jaxpr/dot_general | solution.py:27
  193.6 9.7 %fusion.8 = f32[1,100,1024]{2,1,0:T(8,128)S(1)} fusion(bf16[4096,1024]{1,0:T(8,128)(2,1)} %all-gather.5.cloned.1.call-done, f32[4096]{0:T(1024)S(1)} %bitcast.37, f32[100,1024]{1,0:T(8,128)S(1)} %fusion.9, f32[100,1024]{1,0:T(8,128)S(1)} %fusion.10, f32[100,1024]{1,0:T(8,128)S(1)} %fusion.11, f32[1,100,1024]{2,0,1:T(1,128)S(1)} %copy-done.1), kind=kOutput, calls=%fused_computation.14 | convolution fusion | flops 1679462400 | bytes 10452992 | tf_op jit(solution)/shard_map/while/body/eval_jaxpr/dot_general | solution.py:27
  203.3 1.2 copy.9
  (3 shorter events, 0.0 us)
Async XLA Ops:
  7.2 105.9 %copy-start = (bf16[64,4096]{1,0:T(8,128)(2,1)S(1)}, bf16[64,4096]{1,0:T(8,128)(2,1)}, u32[]{:S(2)}) copy-start(bf16[64,4096]{1,0:T(8,128)(2,1)} %param.10) | copy-start | bytes 1572868
  7.2 106.1 %copy-start.3 = (f32[16,64]{1,0:T(8,128)S(1)}, f32[16,64]{1,0:T(8,128)}, u32[]{:S(2)}) copy-start(f32[16,64]{1,0:T(8,128)} %param.11) | copy-start | bytes 12292
  7.2 80.0 %all-gather.5.cloned.1.call-start = ((), (), s32[]{:S(2)}) async-start(), calls=%async_computation | async-start | bytes 8912896 | tf_op jit(solution)/shard_map/all_gather | solution.py:37
  7.9 156.5 %copy-start.1 = (f32[1,100,1024]{2,0,1:T(1,128)S(1)}, f32[1,100,1024]{2,0,1:T(1,128)}, u32[]{:S(2)}) copy-start(f32[1,100,1024]{2,0,1:T(1,128)} %param.6) | copy-start | bytes 1228804
  7.9 154.1 %all-gather.7.cloned.1.call-start = ((), (), s32[]{:S(2)}) async-start(), calls=%async_computation.1 | async-start | bytes 4456448 | tf_op jit(solution)/shard_map/all_gather | solution.py:45
  113.3 60.8 %copy-start.2 = (f32[16,64]{1,0:T(8,128)}, f32[16,64]{1,0:T(8,128)S(1)}, u32[]{:S(2)}) copy-start(f32[16,64]{1,0:T(8,128)S(1)} %fusion.28) | copy-start | bytes 12292
Sparse Core Ops, SparseCore 0:
  10.2 77.0 all-gather.4
  114.4 47.5 all-gather.6
